TPU v7x, 256 devices: a whole 4x4x8 slice. The times are simulated.
256 devices in a mesh: occ: 16 (over z_lo, y), aux: 16 (over z_hi, x, core).
Axes of the slice: x: 4, y: 4, z: 8 (z_hi: 2, z_lo: 4; z = z_hi * 4 + z_lo), core: 2. Of those that a mesh axis runs over, the one named last changes fastest.
Arguments:
- factors: bfloat16 [8192, 32, 1024], P('aux', 'occ'), may hold values from -16 to 16
- partner: bfloat16 [8192, 1024], P('aux', 'occ'), may hold values from -0.09375 to 0.09375
- occupied_energy: float32 [32], P('occ'), may hold values from -2 to -0.5
- partner_energy: float32 [1], replicated, may hold values from -3 to -0.3
- virtual_energy: float32 [1024], replicated, may hold values from 0.2 to 3
Outputs:
- amplitudes: bfloat16 [32768, 1024], P(('occ', 'aux'))
- density_factors: bfloat16 [8192, 32, 1024], P('aux', 'occ')
All inputs are finite; a program needn't handle non-finite values.
Results may differ from a plain program's by a relative error of at most 0.015.
Values may be sent and summed in bfloat16 or wider, within the bound.
A program may use at most 64 MiB of HBM per device.

v0:
```python
import jax
import jax.numpy as jnp
from jax import lax
from jax.sharding import PartitionSpec as P


def lookup(entries, indices):
    positions = jnp.arange(entries.shape[0], dtype=jnp.int32)
    matches = indices[:, None] == positions[None, :]
    return jnp.sum(jnp.where(matches, entries[None, :], 0.0), axis=1)


def shards(factors, partner, occupied_energy, partner_energy, virtual_energy):
    aux_rows, local_occ, virt_count = factors.shape
    partner_full = lax.all_gather(partner, "occ", axis=1, tiled=True)
    flat_factors = factors.reshape(aux_rows, local_occ * virt_count)
    total_rows = local_occ * virt_count
    row_share = total_rows // lax.axis_size("aux")
    own_first = lax.axis_index("aux") * row_share
    integrals = lax.psum_scatter(
        lax.dot_general(
            flat_factors, partner_full, (((0,), (0,)), ((), ())), preferred_element_type=jnp.float32
        ).astype(jnp.bfloat16),
        "aux",
        scatter_dimension=0,
        tiled=True,
    ).astype(jnp.float32)
    row_ids = own_first + jnp.arange(row_share, dtype=jnp.int32)
    occ_part = lookup(occupied_energy, row_ids // virt_count)
    virt_part = lookup(virtual_energy, row_ids % virt_count)
    divisor = virt_part[:, None] + virtual_energy[None, :] - occ_part[:, None] - partner_energy[0]
    amp_shard = (-integrals / divisor).astype(jnp.bfloat16)
    amp_full = lax.all_gather(amp_shard, "aux", axis=0, tiled=True)
    amp_cube = amp_full.reshape(local_occ, virt_count, virt_count)
    direct = jnp.einsum("qb,iab->qia", partner_full, amp_cube, preferred_element_type=jnp.float32)
    swapped = jnp.einsum("qb,iba->qia", partner_full, amp_cube, preferred_element_type=jnp.float32)
    density = (2.0 * direct - swapped).astype(jnp.bfloat16)
    return (amp_shard, density)


def solution(mesh):
    return jax.shard_map(
        shards,
        mesh=mesh,
        in_specs=(P("aux", "occ", None), P("aux", "occ"), P("occ"), P(), P()),
        out_specs=(P(("occ", "aux"), None), P("aux", "occ", None)),
        check_vma=False,
    )
```

profile of v0, /device:TPU:1, one launch (start us, length us, event | category | flops | bytes accessed | tf_op | source)
XLA Modules:
  0.0 296.8 jit_solution(7066231302340933514)
XLA Ops:
  7.2 0.0 all-gather.3.cloned.1.call-start
  7.2 0.7 all-gather.3.cloned.1.call-update
  7.9 0.0 reduce-scatter.2.cloned.1.call-start
  7.9 2.2 copy.12
  10.1 73.7 %all-gather.3.cloned.1.call-done = bf16[512,1024]{0,1:T(8,128)(2,1)} async-done(((bf16[512,64]{0,1:T(8,128)(2,1)}), bf16[512,1024]{0,1:T(8,128)(2,1)}) %all-gather.3.cloned.1.call-update) | async-done | bytes 1048592 | tf_op jit(solution)/shard_map/all_gather | solution.py:15
  83.9 5.6 %convolution_convert_fusion = bf16[2048,1024]{1,0:T(8,128)(2,1)} fusion(bf16[512,2048]{1,0:T(8,128)(2,1)S(1)} %bitcast.17, bf16[512,1024]{0,1:T(8,128)(2,1)} %all-gather.3.cloned.1.call-done), kind=kOutput, calls=%fused_computation.1 | convolution fusion | flops 2149580800 | bytes 7340032 | tf_op jit(solution)/shard_map/dot_general | solution.py:21
  89.4 0.0 copy-start.3
  89.4 0.0 copy-start
  89.4 0.0 copy-start.2
  89.4 0.0 reduce-scatter.2.cloned.1.call-update
  89.5 0.0 all-gather.5.cloned.1.call-start
  90.3 0.0 copy-done.3
  90.3 0.1 fusion.4
  90.4 0.0 copy-done
  90.4 0.2 select_reduce_fusion
  90.6 110.0 %reduce-scatter.2.cloned.1.call-done = bf16[128,1024]{1,0:T(8,128)(2,1)} async-done(((bf16[2048,1024]{1,0:T(8,128)(2,1)}), bf16[128,1024]{1,0:T(8,128)(2,1)}) %reduce-scatter.2.cloned.1.call-update) | async-done | bytes 262160 | tf_op jit(solution)/shard_map/reduce_scatter | solution.py:20
  200.5 1.9 divide_convert_fusion
  202.4 0.0 all-gather.5.cloned.1.call-update
  202.4 76.8 %all-gather.5.cloned.1.call-done = bf16[2048,1024]{1,0:T(8,128)(2,1)} async-done(((bf16[128,1024]{1,0:T(8,128)(2,1)}), bf16[2048,1024]{1,0:T(8,128)(2,1)}) %all-gather.5.cloned.1.call-update) | async-done | bytes 4194320 | tf_op jit(solution)/shard_map/all_gather | solution.py:33
  279.2 0.0 copy-done.2
  279.2 0.0 copy-start.1
  279.2 4.7 %fusion.1 = f32[2,1024,512]{2,1,0:T(8,128)S(1)} fusion(bf16[2,1024,1024]{2,1,0:T(8,128)(2,1)} %bitcast.18, bf16[512,1024]{0,1:T(8,128)(2,1)S(1)} %copy-done.2), kind=kOutput, calls=%fused_computation.3 | convolution fusion | flops 2147483648 | bytes 9437184 | tf_op jit(solution)/shard_map/qb,iba->qia/dot_general | solution.py:36
  283.9 0.0 copy-done.1
  284.0 2.3 fusion
  286.3 3.9 %copy.10 = bf16[512,2,1024]{2,1,0:T(2,128)(2,1)} copy(bf16[512,2,1024]{0,2,1:T(8,128)(2,1)S(1)} %fusion) | data formatting | bytes 4194304
  (1 shorter events, 0.0 us)
Async XLA Ops:
  7.2 76.7 %all-gather.3.cloned.1.call-start = ((), (), s32[]{:S(2)}) async-start(), calls=%async_computation.1 | async-start | bytes 1114112 | tf_op jit(solution)/shard_map/all_gather | solution.py:15
  7.9 192.6 %reduce-scatter.2.cloned.1.call-start = ((), (), s32[]{:S(2)}) async-start(), calls=%async_computation.2 | async-start | bytes 4456448 | tf_op jit(solution)/shard_map/reduce_scatter | solution.py:20
  89.4 0.8 copy-start.3
  89.4 0.9 copy-start
  89.4 189.8 %copy-start.2 = (bf16[512,1024]{0,1:T(8,128)(2,1)S(1)}, bf16[512,1024]{0,1:T(8,128)(2,1)}, u32[]{:S(2)}) copy-start(bf16[512,1024]{0,1:T(8,128)(2,1)} %all-gather.3.cloned.1.call-done) | copy-start | bytes 3145732
  89.5 189.7 %all-gather.5.cloned.1.call-start = ((), (), s32[]{:S(2)}) async-start(), calls=%async_computation.3 | async-start | bytes 4456448 | tf_op jit(solution)/shard_map/all_gather | solution.py:33
  279.2 4.7 %copy-start.1 = (bf16[2048,1024]{1,0:T(8,128)(2,1)S(1)}, bf16[2048,1024]{1,0:T(8,128)(2,1)}, u32[]{:S(2)}) copy-start(bf16[2048,1024]{1,0:T(8,128)(2,1)} %all-gather.5.cloned.1.call-done) | copy-start | bytes 12582916
Sparse Core Ops, SparseCore 0:
  9.8 74.0 all-gather.2
  89.6 110.8 reduce-scatter.1
  203.8 75.3 all-gather.4
where the time goes:
time: 297 us
  waiting for transfers between devices  261 us (88%)
  between operations  14.5 us (5%)
  matrix products  12.6 us (4%)
  local copies, waits for them, and re-layouts  6.14 us (2%)
    reduce_scatter x1, waiting for transfers between devices, shards(): lax.psum_scatter(lax.dot_general(flat_factors, partner_full, (((0,), (0,)...  110 us
    all_gather x1, waiting for transfers between devices, shards(): amp_full = lax.all_gather(amp_shard, 'aux', axis=0, tiled=True)  76.8 us
    all_gather x1, waiting for transfers between devices, shards(): partner_full = lax.all_gather(partner, 'occ', axis=1, tiled=True)  73.7 us
    unnamed x10, local copies, waits for them, and re-layouts  6.14 us
  transfers between devices with their start and end apart: 3, of which 3 were waited for; matrix products, arithmetic and copies ran while one was open for 1% of the time, Pallas kernels for 0%

commit v1 on v0

--- a/solution.py
+++ b/solution.py
@@ -12,7 +12,9 @@
 
 def shards(factors, partner, occupied_energy, partner_energy, virtual_energy):
     aux_rows, local_occ, virt_count = factors.shape
-    partner_full = lax.all_gather(partner, "occ", axis=1, tiled=True)
+    partner_full = jnp.concatenate(
+        lax.all_to_all(jnp.stack([partner] * lax.axis_size("occ")), "occ", 0, 0), axis=1
+    )
     flat_factors = factors.reshape(aux_rows, local_occ * virt_count)
     total_rows = local_occ * virt_count
     row_share = total_rows // lax.axis_size("aux")

time: 297 us -> 249 us (0.84)
  waiting for transfers between devices: 261 us -> 202 us
  starting transfers between devices: 0.12 us -> 9.26 us
    all_gather x1 -> x0, waiting for transfers between devices: 73.7 us -> none  [shards(): partner_full = lax.all_gather(partner, 'occ', axis=1, tiled=True)]
    all_to_all x0 -> x1, waiting for transfers between devices: none -> 20.4 us  [shards(): lax.all_to_all(jnp.stack([partner] * lax.axis_size('occ')), 'occ', 0, 0)]
    all_to_all x0 -> x1, starting transfers between devices: none -> 9.17 us  [shards(): lax.all_to_all(jnp.stack([partner] * lax.axis_size('occ')), 'occ', 0, 0)]
    reduce_scatter x1, waiting for transfers between devices: 110 us -> 105 us  [shards(): lax.psum_scatter(lax.dot_general(flat_factors, partner_full, (((0,), (0,)...]
where the time goes in v1:
time: 249 us
  waiting for transfers between devices  202 us (81%)
  between operations  14.8 us (6%)
  matrix products  13 us (5%)
  starting transfers between devices  9.26 us (4%)
  local copies, waits for them, and re-layouts  7.94 us (3%)
    reduce_scatter x1, waiting for transfers between devices, shards(): lax.psum_scatter(lax.dot_general(flat_factors, partner_full, (((0,), (0,)...  105 us
    all_gather x1, waiting for transfers between devices, shards(): amp_full = lax.all_gather(amp_shard, 'aux', axis=0, tiled=True)  76.7 us
    all_to_all x1, waiting for transfers between devices, shards(): lax.all_to_all(jnp.stack([partner] * lax.axis_size('occ')), 'occ', 0, 0)  20.4 us
    all_to_all x1, starting transfers between devices, shards(): lax.all_to_all(jnp.stack([partner] * lax.axis_size('occ')), 'occ', 0, 0)  9.17 us
    dot_general x1, matrix products, shards(): lax.dot_general(flat_factors, partner_full, (((0,), (0,)), ((), ())), pre...  5.93 us
    unnamed x10, local copies, waits for them, and re-layouts  5.89 us
  transfers between devices with their start and end apart: 3, of which 3 were waited for; matrix products, arithmetic and copies ran while one was open for 1% of the time, Pallas kernels for 0%

profile of v1, /device:TPU:1, one launch (start us, length us, event | category | flops | bytes accessed | tf_op | source)
XLA Modules:
  0.0 248.8 jit_solution(5234044562125168430)
XLA Ops:
  7.2 0.0 copy-start
  7.2 2.1 stack.2
  9.2 9.2 %all-to-all-start = ((bf16[16,512,64]{1,2,0:T(8,128)(2,1)}), bf16[16,512,64]{1,2,0:T(8,128)(2,1)S(1)}, u32[]{:S(2)}, u32[]{:S(2)}) async-start(bf16[16,512,64]{1,2,0:T(8,128)(2,1)} %stack.2), calls=%async_computation | async-start | bytes 2097152 | tf_op jit(solution)/shard_map/all_to_all | solution.py:16
  18.4 0.0 reduce-scatter.2.cloned.1.call-start
  18.5 0.0 copy-done
  18.5 1.9 copy.23
  20.4 20.4 %all-to-all-done = bf16[16,512,64]{1,2,0:T(8,128)(2,1)S(1)} async-done(((bf16[16,512,64]{1,2,0:T(8,128)(2,1)}), bf16[16,512,64]{1,2,0:T(8,128)(2,1)S(1)}, u32[]{:S(2)}, u32[]{:S(2)}) %all-to-all-start) | async-done | bytes 1048608 | tf_op jit(solution)/shard_map/all_to_all | solution.py:16
  40.8 5.9 %convolution_convert_fusion = bf16[2048,1024]{1,0:T(8,128)(2,1)} fusion(bf16[512,2048]{1,0:T(8,128)(2,1)} %bitcast.20, bf16[512,1024]{0,1:T(8,128)(2,1)S(1)} %bitcast.21), kind=kOutput, calls=%fused_computation.1 | convolution fusion | flops 2149580800 | bytes 7340032 | tf_op jit(solution)/shard_map/dot_general | solution.py:23
  46.7 0.0 copy-start.3
  46.7 0.0 copy-start.1
  46.7 0.0 reduce-scatter.2.cloned.1.call-update
  46.7 0.0 all-gather.2.cloned.1.call-start
  47.4 0.0 copy-done.3
  47.5 0.1 fusion.1
  47.5 0.0 copy-done.1
  47.5 0.2 select_reduce_fusion
  47.7 104.6 %reduce-scatter.2.cloned.1.call-done = bf16[128,1024]{1,0:T(8,128)(2,1)} async-done(((bf16[2048,1024]{1,0:T(8,128)(2,1)}), bf16[128,1024]{1,0:T(8,128)(2,1)}) %reduce-scatter.2.cloned.1.call-update) | async-done | bytes 262160 | tf_op jit(solution)/shard_map/reduce_scatter | solution.py:22
  152.3 1.9 divide_convert_fusion
  154.2 0.0 all-gather.2.cloned.1.call-update
  154.2 76.7 %all-gather.2.cloned.1.call-done = bf16[2048,1024]{1,0:T(8,128)(2,1)} async-done(((bf16[128,1024]{1,0:T(8,128)(2,1)}), bf16[2048,1024]{1,0:T(8,128)(2,1)}) %all-gather.2.cloned.1.call-update) | async-done | bytes 4194320 | tf_op jit(solution)/shard_map/all_gather | solution.py:35
  230.9 0.0 copy-start.2
  230.9 4.7 %fusion.2 = f32[2,1024,512]{2,1,0:T(8,128)S(1)} fusion(bf16[2,1024,1024]{2,1,0:T(8,128)(2,1)} %bitcast.24, bf16[512,1024,1]{0,1,2:T(8,128)(2,1)S(1)} %bitcast.22), kind=kOutput, calls=%fused_computation.14 | convolution fusion | flops 2147483648 | bytes 9437184 | tf_op jit(solution)/shard_map/qb,iba->qia/dot_general | solution.py:38
  235.7 0.0 copy-done.2
  235.7 2.3 fusion
  238.0 3.9 %copy.17 = bf16[512,2,1024]{2,1,0:T(2,128)(2,1)} copy(bf16[512,2,1024]{0,2,1:T(8,128)(2,1)S(1)} %fusion) | data formatting | bytes 4194304
  (1 shorter events, 0.0 us)
Async XLA Ops:
  7.2 11.3 %copy-start = (bf16[512,2,1024]{2,1,0:T(2,128)(2,1)S(1)}, bf16[512,2,1024]{2,1,0:T(2,128)(2,1)}, u32[]{:S(2)}) copy-start(bf16[512,2,1024]{2,1,0:T(2,128)(2,1)} %param.5) | copy-start | bytes 6291460
  9.2 31.5 %all-to-all-start = ((bf16[16,512,64]{1,2,0:T(8,128)(2,1)}), bf16[16,512,64]{1,2,0:T(8,128)(2,1)S(1)}, u32[]{:S(2)}, u32[]{:S(2)}) async-start(bf16[16,512,64]{1,2,0:T(8,128)(2,1)} %stack.2), calls=%async_computation | async-start | bytes 2097152 | tf_op jit(solution)/shard_map/all_to_all | solution.py:16
  18.4 133.9 %reduce-scatter.2.cloned.1.call-start = ((), (), s32[]{:S(2)}) async-start(), calls=%async_computation.2 | async-start | bytes 4456448 | tf_op jit(solution)/shard_map/reduce_scatter | solution.py:22
  46.7 0.8 copy-start.3
  46.7 0.8 copy-start.1
  46.7 184.2 %all-gather.2.cloned.1.call-start = ((), (), s32[]{:S(2)}) async-start(), calls=%async_computation.3 | async-start | bytes 4456448 | tf_op jit(solution)/shard_map/all_gather | solution.py:35
  230.9 4.7 %copy-start.2 = (bf16[2048,1024]{1,0:T(8,128)(2,1)S(1)}, bf16[2048,1024]{1,0:T(8,128)(2,1)}, u32[]{:S(2)}) copy-start(bf16[2048,1024]{1,0:T(8,128)(2,1)} %all-gather.2.cloned.1.call-done) | copy-start | bytes 12582916
Sparse Core Ops, SparseCore 0:
  46.8 105.4 reduce-scatter.1
  155.6 75.2 all-gather.1
